TPU v7x, 512 devices: a whole 4x8x8 slice. The times are simulated.
512 devices in a mesh: shell: 8 (over z), row: 4 (over x_hi, core), col: 16 (over x_lo, y).
Axes of the slice: x: 4 (x_hi: 2, x_lo: 2; x = x_hi * 2 + x_lo), y: 8, z: 8, core: 2. Of those that a mesh axis runs over, the one named last changes fastest.
Arguments:
- left_basis: bfloat16 [2, 4096, 6144], P(None, 'row', 'shell'), may hold values from -6 to 6
- right_basis: bfloat16 [2, 6144, 8192], P(None, 'shell', 'col'), may hold values from -0.078125 to 0.078125
- point_weight: float32 [6144], P('shell'), may hold values from 0.3 to 3
- shell_index: int32 [6144], P('shell'), may hold values from 0 to 11
- green_table: float32 [12, 2], replicated, may hold values from -4 to 4
- pivot_rows: int32 [512], replicated, may hold values from 0 to 4095, as said below
- diag_inverse: bfloat16 [2, 512, 512], replicated, may hold values from -0.005859375 to 0.005859375
Outputs:
- factored: float32 [2, 4, 8, 128, 8192], P(None, 'row', 'shell', None, 'col')
Inputs may be any that keep to these rules, and one draw needn't show every extreme that they name: `pivot_rows`: 512 distinct matrix rows.
All inputs are finite; a program needn't handle non-finite values.
Results may differ from a plain program's by a relative error of at most 0.0056.
Values may be sent and summed in bfloat16 or wider, within the bound.
No kernel may reach another device: no remote copies, remote signals or barrier semaphores. Data moves between devices by JAX's collectives and lax.ppermute only.
A program may use at most 128 MiB of HBM per device.

v0:
```python
import jax
import jax.numpy as jnp
from jax import lax
from jax.sharding import PartitionSpec as P


def broadcast(block, axis, source):
    block = jnp.where(lax.axis_index(axis) == source, block, jnp.zeros_like(block))
    return lax.psum(block, axis)


def complex_block(real_part, imag_part):
    upper_half = jnp.concatenate([real_part, imag_part], axis=1)
    lower_half = jnp.concatenate([-imag_part, real_part], axis=1)
    return jnp.concatenate([upper_half, lower_half], axis=0)


def weigh_points(right_basis, point_weight, shell_index, green_table):
    shells_count = green_table.shape[0]
    matches = shell_index[:, None] == jnp.arange(shells_count, dtype=jnp.int32)[None, :]
    green_real = jnp.sum(jnp.where(matches, green_table[None, :, 0], 0.0), axis=1)
    green_imag = jnp.sum(jnp.where(matches, green_table[None, :, 1], 0.0), axis=1)
    weight_real = point_weight * green_real
    weight_imag = point_weight * green_imag
    basis_real = right_basis[0].astype(jnp.float32)
    basis_imag = right_basis[1].astype(jnp.float32)
    weighted_real = (weight_real[:, None] * basis_real - weight_imag[:, None] * basis_imag).astype(
        jnp.bfloat16
    )
    weighted_imag = (weight_real[:, None] * basis_imag + weight_imag[:, None] * basis_real).astype(
        jnp.bfloat16
    )
    return (weighted_real, weighted_imag)


def reduce_tiles(term_rows, owned_rows):
    return lax.psum_scatter(
        term_rows(jnp.int32(0), owned_rows * lax.axis_size("shell")),
        "shell",
        scatter_dimension=0,
        tiled=True,
    )


def pick_rows(matrix_rows, pivot_rows, row_base):
    held_rows = matrix_rows.shape[0]
    local_index = pivot_rows - row_base
    inside = (local_index >= 0) & (local_index < held_rows)
    picked = jnp.take(matrix_rows, jnp.clip(local_index, 0, held_rows - 1), axis=0)
    return jnp.where(inside[:, None], picked, 0.0)


def select_pivots(coupling, pivot_rows, row_base):
    picked = pick_rows(coupling, pivot_rows, row_base).astype(jnp.bfloat16)
    return lax.psum(picked, ("shell", "row")).astype(jnp.float32).astype(jnp.bfloat16)


def body(left_basis, right_basis, point_weight, shell_index, green_table, pivot_rows, diag_inverse):
    shells = lax.axis_size("shell")
    owned_rows = left_basis.shape[1] // shells
    panel_width = right_basis.shape[2]
    weighted_real, weighted_imag = weigh_points(right_basis, point_weight, shell_index, green_table)
    grid_row = lax.axis_index("row")
    shell_rank = lax.axis_index("shell")
    row_base = (grid_row * shells + shell_rank) * owned_rows
    left_stack = jnp.concatenate([left_basis[0], left_basis[1]], axis=1)
    right_stack = complex_block(weighted_real, weighted_imag)

    def from_bases(first_row, row_count):
        return jnp.dot(left_stack, right_stack, preferred_element_type=jnp.float32)

    coupling = reduce_tiles(from_bases, owned_rows)
    pivot_sum = select_pivots(coupling, pivot_rows, row_base)
    panel_real = coupling[:, :panel_width]
    panel_imag = coupling[:, panel_width:]
    inverse_real = diag_inverse[0].astype(jnp.float32)
    inverse_imag = diag_inverse[1].astype(jnp.float32)
    highest = lax.Precision.HIGHEST
    mult_real = (
        jnp.dot(panel_real, inverse_real, precision=highest, preferred_element_type=jnp.float32)
        - jnp.dot(panel_imag, inverse_imag, precision=highest, preferred_element_type=jnp.float32)
    ).astype(jnp.bfloat16)
    mult_imag = (
        jnp.dot(panel_real, inverse_imag, precision=highest, preferred_element_type=jnp.float32)
        + jnp.dot(panel_imag, inverse_real, precision=highest, preferred_element_type=jnp.float32)
    ).astype(jnp.bfloat16)
    multipliers = jnp.concatenate([mult_real, mult_imag], axis=1)
    multipliers = broadcast(multipliers, "col", 0)
    pivot_block = complex_block(pivot_sum[:, :panel_width], pivot_sum[:, panel_width:])
    update = jnp.dot(multipliers, pivot_block, preferred_element_type=jnp.float32)
    updated = coupling - update
    return jnp.stack([updated[:, :panel_width], updated[:, panel_width:]]).reshape(
        2, 1, 1, owned_rows, panel_width
    )


def solution(mesh):
    return jax.shard_map(
        body,
        mesh=mesh,
        in_specs=(
            P(None, "row", "shell"),
            P(None, "shell", "col"),
            P("shell"),
            P("shell"),
            P(),
            P(),
            P(),
        ),
        out_specs=P(None, "row", "shell", None, "col"),
        check_vma=False,
    )
```

profile of v0, /device:TPU:4, one launch (start us, length us, event | category | flops | bytes accessed | tf_op | source)
XLA Modules:
  0.0 509.2 jit_solution(4400206457405959289)
XLA Ops:
  6.5 0.8 slice_bitcast_fusion.4
  7.4 0.8 select_reduce_fusion.1
  8.1 0.7 fusion.44
  8.8 1.9 fusion.42
  10.8 0.4 fusion.18
  11.2 0.2 slice_bitcast_fusion.1
  11.4 5.3 %fusion = f32[1024,1024]{1,0:T(8,128)} fusion(bf16[1024,768]{1,0:T(8,128)(2,1)S(1)} %get-tuple-element.12, bf16[1024,768]{1,0:T(8,128)(2,1)S(1)} %get-tuple-element.11, bf16[768,512]{1,0:T(8,128)(2,1)S(1)} %fusion.18, bf16[768,512]{1,0:T(8,128)(2,1)S(1)} %get-tuple-element.9, bf16[768,512]{1,0:T(8,128)(2,1)S(1)} %get-tuple-element.10), kind=kOutput, calls=%fused_computation.1 | convolution fusion | flops 3240099840 | bytes 9699328 | tf_op jit(solution)/shard_map/dot_general | solution.py:70
  16.8 0.0 all-reduce.5.cloned.1.call-start
  16.8 0.6 copy-done.5
  17.4 62.8 %reduce-scatter.2.cloned.1.call-done = f32[128,1024]{1,0:T(8,128)} async-done(((f32[1024,1024]{1,0:T(8,128)}), f32[128,1024]{1,0:T(8,128)}) %reduce-scatter.2.cloned.1.call-update) | async-done | bytes 524304 | tf_op jit(solution)/shard_map/reduce_scatter | solution.py:37
  80.3 3.8 gather_fusion
  84.1 1.4 select_convert_fusion
  85.4 0.0 all-reduce.3.cloned.1.call-start
  85.5 0.2 copy-done.2
  85.7 0.4 fusion.30
  86.1 0.4 fusion.26
  86.4 0.4 fusion.24
  86.8 0.4 fusion.25
  87.2 0.8 maximum_select_fusion
  88.0 267.2 %all-reduce.5.cloned.1.call-done = bf16[512,1024]{1,0:T(8,128)(2,1)} async-done(((bf16[512,1024]{1,0:T(8,128)(2,1)}), bf16[512,1024]{1,0:T(8,128)(2,1)}) %all-reduce.5.cloned.1.call-update) | async-done | bytes 1048592 | tf_op jit(solution)/shard_map/psum | solution.py:55
  355.2 1.4 slice_negate_fusion
  356.6 143.8 %all-reduce.3.cloned.1.call-done = bf16[128,1024]{1,0:T(8,128)(2,1)} async-done(((bf16[128,1024]{1,0:T(8,128)(2,1)}), bf16[128,1024]{1,0:T(8,128)(2,1)}) %all-reduce.3.cloned.1.call-update) | async-done | bytes 262160 | tf_op jit(solution)/shard_map/psum | solution.py:9
  500.4 1.4 fusion.21
  501.8 0.8 maximum_bitcast_fusion
  (17 shorter events, 0.1 us)
Async XLA Ops:
  6.5 4.2 copy-start.1
  6.5 73.7 %reduce-scatter.2.cloned.1.call-start = ((), (), s32[]{:S(2)}) async-start(), calls=%async_computation.1 | async-start | bytes 4718592 | tf_op jit(solution)/shard_map/reduce_scatter | solution.py:37
  8.8 2.4 copy-start.3
  16.7 0.7 copy-start.5
  16.8 338.4 %all-reduce.5.cloned.1.call-start = ((), (), s32[]{:S(2)}) async-start(), calls=%async_computation.3 | async-start | bytes 2097152 | tf_op jit(solution)/shard_map/psum | solution.py:55
  84.0 1.5 copy-start
  84.0 1.6 copy-start.2
  85.4 414.9 %all-reduce.3.cloned.1.call-start = ((), (), s32[]{:S(2)}) async-start(), calls=%async_computation.2 | async-start | bytes 524288 | tf_op jit(solution)/shard_map/psum | solution.py:9
  355.2 145.2 %copy-start.4 = (bf16[512,1024]{1,0:T(8,128)(2,1)S(1)}, bf16[512,1024]{1,0:T(8,128)(2,1)}, u32[]{:S(2)}) copy-start(bf16[512,1024]{1,0:T(8,128)(2,1)} %all-reduce.5.cloned.1.call-done) | copy-start | bytes 3145732
Sparse Core Ops, SparseCore 0:
  16.9 63.3 reduce-scatter.1
  85.6 269.6 all-reduce.4
  358.4 141.9 all-reduce.2
where the time goes:
time: 509 us
  waiting for transfers between devices  474 us (93%)
  between operations  13.2 us (3%)
  matrix products  8.23 us (2%)
  other arithmetic  8.1 us (2%)
  local copies, waits for them, and re-layouts  5.65 us (1%)
    psum x1, waiting for transfers between devices, select_pivots(): lax.psum(picked, ('shell', 'row')).astype(jnp.float32).astype(jnp.bfloat16)  267 us
    psum x1, waiting for transfers between devices, broadcast(): return lax.psum(block, axis)  144 us
    reduce_scatter x1, waiting for transfers between devices, reduce_tiles(): lax.psum_scatter(term_rows(jnp.int32(0), owned_rows * lax.axis_size('shel...  62.8 us
  transfers between devices with their start and end apart: 3, of which 3 were waited for; matrix products, arithmetic and copies ran while one was open for 1% of the time, Pallas kernels for 0%

commit v1 on v0

--- a/solution.py
+++ b/solution.py
@@ -1,7 +1,17 @@
+import functools
 import jax
 import jax.numpy as jnp
 from jax import lax
 from jax.sharding import PartitionSpec as P
+
+
+def steps_all_use(s0, mesh_name, row_axis):
+    for idx in (mesh_name, row_axis):
+        s0 = lax.psum(s0, axis_name=idx)
+    return s0
+
+
+series_take = functools.partial(steps_all_use, mesh_name="shell", row_axis="row")
 
 
 def broadcast(block, axis, source):
@@ -52,7 +62,7 @@
 
 def select_pivots(coupling, pivot_rows, row_base):
     picked = pick_rows(coupling, pivot_rows, row_base).astype(jnp.bfloat16)
-    return lax.psum(picked, ("shell", "row")).astype(jnp.float32).astype(jnp.bfloat16)
+    return series_take(picked).astype(jnp.float32).astype(jnp.bfloat16)
 
 
 def body(left_basis, right_basis, point_weight, shell_index, green_table, pivot_rows, diag_inverse):

time: 509 us -> 374 us (0.73)
  waiting for transfers between devices: 474 us -> 338 us
    psum x1 -> x2, waiting for transfers between devices: 267 us -> 133 us  [steps_all_use(): s0 = lax.psum(s0, axis_name=idx)]
  transfers between devices with their start and end apart: 3 -> 4, of which waited for: 3 -> 4; matrix products, arithmetic and copies ran while one was open for 1% -> 1% of each run, Pallas kernels for 0% -> 0%
where the time goes in v1:
time: 374 us
  waiting for transfers between devices  338 us (90%)
  between operations  13.3 us (4%)
  matrix products  8.23 us (2%)
  other arithmetic  8.1 us (2%)
  local copies, waits for them, and re-layouts  5.46 us (1%)
    psum x1, waiting for transfers between devices, broadcast(): return lax.psum(block, axis)  142 us
    psum x2, waiting for transfers between devices, steps_all_use(): s0 = lax.psum(s0, axis_name=idx)  133 us
    reduce_scatter x1, waiting for transfers between devices, reduce_tiles(): lax.psum_scatter(term_rows(jnp.int32(0), owned_rows * lax.axis_size('shel...  62.8 us
  transfers between devices with their start and end apart: 4, of which 4 were waited for; matrix products, arithmetic and copies ran while one was open for 1% of the time, Pallas kernels for 0%

profile of v1, /device:TPU:4, one launch (start us, length us, event | category | flops | bytes accessed | tf_op | source)
XLA Modules:
  0.0 373.6 jit_solution(9171483931521371890)
XLA Ops:
  6.5 0.8 slice_bitcast_fusion.4
  7.4 0.8 select_reduce_fusion.1
  8.1 0.7 fusion.44
  8.8 1.9 fusion.42
  10.8 0.4 fusion.18
  11.2 0.2 slice_bitcast_fusion.1
  11.4 5.3 %fusion = f32[1024,1024]{1,0:T(8,128)} fusion(bf16[1024,768]{1,0:T(8,128)(2,1)S(1)} %get-tuple-element.12, bf16[1024,768]{1,0:T(8,128)(2,1)S(1)} %get-tuple-element.11, bf16[768,512]{1,0:T(8,128)(2,1)S(1)} %fusion.18, bf16[768,512]{1,0:T(8,128)(2,1)S(1)} %get-tuple-element.9, bf16[768,512]{1,0:T(8,128)(2,1)S(1)} %get-tuple-element.10), kind=kOutput, calls=%fused_computation.1 | convolution fusion | flops 3240099840 | bytes 9699328 | tf_op jit(solution)/shard_map/dot_general | solution.py:80
  16.8 0.0 all-reduce.6.cloned.1.call-start
  16.8 0.6 copy-done.5
  17.4 62.8 %reduce-scatter.2.cloned.1.call-done = f32[128,1024]{1,0:T(8,128)} async-done(((f32[1024,1024]{1,0:T(8,128)}), f32[128,1024]{1,0:T(8,128)}) %reduce-scatter.2.cloned.1.call-update) | async-done | bytes 524304 | tf_op jit(solution)/shard_map/reduce_scatter | solution.py:47
  80.3 3.8 %gather_fusion = bf16[512,1024]{1,0:T(8,128)(2,1)S(1)} fusion(f32[128,1024]{1,0:T(8,128)} %reduce-scatter.2.cloned.1.call-done, s32[1024]{0:T(1024)S(1)} %pad_clamp_fusion), kind=kCustom, calls=%fused_computation | custom fusion | bytes 2099200 | tf_op jit(solution)/shard_map/jit(_take)/gather | solution.py:59
  84.1 1.4 select_convert_fusion
  85.4 0.0 all-reduce.8.cloned.1.call-start
  85.5 80.4 %all-reduce.6.cloned.1.call-done = bf16[512,1024]{1,0:T(8,128)(2,1)} async-done(((bf16[512,1024]{1,0:T(8,128)(2,1)}), bf16[512,1024]{1,0:T(8,128)(2,1)}) %all-reduce.6.cloned.1.call-update) | async-done | bytes 1048592 | tf_op jit(solution)/shard_map/psum | solution.py:10
  166.0 0.4 fusion.30
  166.3 0.4 fusion.26
  166.7 0.4 fusion.24
  167.1 0.4 fusion.25
  167.5 0.8 maximum_select_fusion
  168.3 52.7 %all-reduce.8.cloned.1.call-done = bf16[512,1024]{1,0:T(8,128)(2,1)} async-done(((bf16[512,1024]{1,0:T(8,128)(2,1)}), bf16[512,1024]{1,0:T(8,128)(2,1)}) %all-reduce.8.cloned.1.call-update) | async-done | bytes 1048592 | tf_op jit(solution)/shard_map/psum | solution.py:10
  221.0 1.4 slice_negate_fusion
  222.3 142.4 %all-reduce.4.cloned.1.call-done = bf16[128,1024]{1,0:T(8,128)(2,1)} async-done(((bf16[128,1024]{1,0:T(8,128)(2,1)}), bf16[128,1024]{1,0:T(8,128)(2,1)}) %all-reduce.4.cloned.1.call-update) | async-done | bytes 262160 | tf_op jit(solution)/shard_map/psum | solution.py:19
  364.8 1.4 fusion.21
  366.2 0.8 maximum_bitcast_fusion
  (20 shorter events, 0.2 us)
Async XLA Ops:
  6.5 4.2 %copy-start.1 = (bf16[2,768,512]{2,1,0:T(8,128)(2,1)S(1)}, bf16[2,768,512]{2,1,0:T(8,128)(2,1)}, u32[]{:S(2)}) copy-start(bf16[2,768,512]{2,1,0:T(8,128)(2,1)} %param.8) | copy-start | bytes 4718596
  6.5 73.7 %reduce-scatter.2.cloned.1.call-start = ((), (), s32[]{:S(2)}) async-start(), calls=%async_computation.1 | async-start | bytes 4718592 | tf_op jit(solution)/shard_map/reduce_scatter | solution.py:47
  8.8 2.4 copy-start.3
  16.7 0.7 copy-start.5
  16.8 149.1 %all-reduce.6.cloned.1.call-start = ((), (), s32[]{:S(2)}) async-start(), calls=%async_computation.3 | async-start | bytes 2097152 | tf_op jit(solution)/shard_map/psum | solution.py:10
  84.0 81.9 %copy-start = (f32[128,1024]{1,0:T(8,128)S(1)}, f32[128,1024]{1,0:T(8,128)}, u32[]{:S(2)}) copy-start(f32[128,1024]{1,0:T(8,128)} %reduce-scatter.2.cloned.1.call-done) | copy-start | bytes 1572868
  84.0 81.9 %copy-start.2 = (bf16[2,512,512]{2,1,0:T(8,128)(2,1)S(1)}, bf16[2,512,512]{2,1,0:T(8,128)(2,1)}, u32[]{:S(2)}) copy-start(bf16[2,512,512]{2,1,0:T(8,128)(2,1)} %param.13) | copy-start | bytes 3145732
  85.4 135.5 %all-reduce.8.cloned.1.call-start = ((), (), s32[]{:S(2)}) async-start(), calls=%async_computation.4 | async-start | bytes 2097152 | tf_op jit(solution)/shard_map/psum | solution.py:10
  165.9 198.9 %all-reduce.4.cloned.1.call-start = ((), (), s32[]{:S(2)}) async-start(), calls=%async_computation.2 | async-start | bytes 524288 | tf_op jit(solution)/shard_map/psum | solution.py:19
  221.0 143.8 %copy-start.4 = (bf16[512,1024]{1,0:T(8,128)(2,1)S(1)}, bf16[512,1024]{1,0:T(8,128)(2,1)}, u32[]{:S(2)}) copy-start(bf16[512,1024]{1,0:T(8,128)(2,1)} %all-reduce.8.cloned.1.call-done) | copy-start | bytes 3145732
Sparse Core Ops, SparseCore 0:
  16.9 63.3 reduce-scatter.1
  85.6 80.2 all-reduce.5
  168.8 52.0 all-reduce.7
  224.0 140.7 all-reduce.3
